TPU v7x, 32 devices: a whole 2x2x4 slice. The times are simulated.
32 devices in a mesh: video: 4 (over x, core), frame: 8 (over z, y).
Axes of the slice: x: 2, y: 2, z: 4, core: 2. Of those that a mesh axis runs over, the one named last changes fastest.
Arguments:
- frames: bfloat16 [32, 1024, 640], P(('video', 'frame')), parts along dimension 0, may hold values from -6 to 6
- ref_rows: bfloat16 [4096, 640], P(('video', 'frame')), parts along dimension 0, may hold values from -6 to 6
- w_query: bfloat16 [640, 640], replicated, may hold values from -1 to 1
- w_key: bfloat16 [640, 640], replicated, may hold values from -1 to 1
- w_value: bfloat16 [640, 640], replicated, may hold values from -0.25 to 0.25
- w_out: bfloat16 [640, 640], replicated, may hold values from -0.25 to 0.25
- w_conv: bfloat16 [3, 640, 640], replicated, may hold values from -0.125 to 0.125
- t_query: bfloat16 [640, 640], replicated, may hold values from -1 to 1
- t_key: bfloat16 [640, 640], replicated, may hold values from -1 to 1
- t_value: bfloat16 [640, 640], replicated, may hold values from -0.25 to 0.25
- t_out: bfloat16 [640, 640], replicated, may hold values from -0.25 to 0.25
Outputs:
- result: bfloat16 [32, 1024, 640], P(('video', 'frame')), parts along dimension 0
There are 4 independent parts, one for each index of `video`. A program takes and returns all parts, laid end to end along the dimension named above; an argument that names none is the same for every part. Nothing has to cross between parts.
All inputs are finite; a program needn't handle non-finite values.
Results may differ from a plain program's by a relative error of at most 0.011.
Values may be sent and summed in bfloat16 or wider, within the bound.
A program may use at most 128 MiB of HBM per device.

v0:
```python
import math
import jax
import jax.numpy as jnp
from jax import lax
from jax.sharding import PartitionSpec as P

HEADS = 10


def padded_2(value, sides, width):
    for axis, dim in sides:
        devices, length = (lax.axis_size(axis), value.shape[dim])
        up = [(i, (i + 1) % devices) for i in range(devices - 1)]
        down = [(j, i) for i, j in up]
        last = lax.slice_in_dim(value, length - width, length, axis=dim)
        leading = lax.slice_in_dim(value, 0, width, axis=dim)
        before = lax.ppermute(last, axis, up)
        after = lax.ppermute(leading, axis, down)
        value = jnp.concatenate([before, value, after], axis=dim)
    return value


def layer_norm(value):
    mean = jnp.mean(value, axis=-1, keepdims=True)
    centered = value - mean
    var = jnp.mean(centered * centered, axis=-1, keepdims=True)
    return centered * lax.rsqrt(var + 1e-05)


def project(rows, weight):
    return jnp.dot(rows, weight, preferred_element_type=jnp.float32).astype(jnp.bfloat16)


def split_heads(value, heads):
    nframes, pixels, width = value.shape
    return value.reshape(nframes, pixels, heads, width // heads).transpose(2, 0, 1, 3)


def temporal_attend(tquery, tkeys, tvalues):
    nframes, pixels, width = tquery.shape
    head_dim = width // HEADS
    shaped_q = tquery.reshape(nframes, pixels, HEADS, head_dim)
    shaped_k = tkeys.reshape(nframes, pixels, HEADS, head_dim)
    shaped_v = tvalues.reshape(nframes, pixels, HEADS, head_dim)
    tscores = jnp.einsum(
        "fnhd,gnhd->nhfg", shaped_q, shaped_k, preferred_element_type=jnp.float32
    ) / math.sqrt(head_dim)
    tpeak = jnp.max(tscores, axis=-1, keepdims=True)
    texpo = jnp.exp(tscores - tpeak)
    ttotal = jnp.sum(texpo, axis=-1)
    tmixed = (
        jnp.einsum(
            "nhfg,gnhd->nhfd",
            texpo.astype(jnp.bfloat16),
            shaped_v,
            preferred_element_type=jnp.float32,
        )
        / ttotal[..., None]
    )
    return tmixed.transpose(2, 0, 1, 3).reshape(nframes, pixels, width).astype(jnp.bfloat16)


def per_device(
    frames, ref_rows, w_query, w_key, w_value, w_out, w_conv, t_query, t_key, t_value, t_out
):
    fdev, pixels, width = frames.shape
    head_dim = width // HEADS
    scale = 1.0 / math.sqrt(head_dim)
    ndev = lax.axis_size("frame")
    group_px = pixels // ndev
    normed = layer_norm(frames.astype(jnp.float32)).astype(jnp.bfloat16).reshape(-1, width)
    query = split_heads(project(normed, w_query).reshape(fdev, pixels, width), HEADS)
    keys = split_heads(project(normed, w_key).reshape(fdev, pixels, width), HEADS)
    values = split_heads(project(normed, w_value).reshape(fdev, pixels, width), HEADS)

    def local_part(args):
        qa, ka, va = args
        scores = jnp.einsum("fqd,fkd->fqk", qa, ka, preferred_element_type=jnp.float32) * scale
        peak = jnp.max(scores, axis=-1)
        expo = jnp.exp(scores - peak[..., None])
        total = jnp.sum(expo, axis=-1)
        accum = jnp.einsum(
            "fqk,fkd->fqd", expo.astype(jnp.bfloat16), va, preferred_element_type=jnp.float32
        )
        return (peak, total, accum)

    start_carry = lax.map(local_part, (query, keys, values))
    ref_keys = project(ref_rows, w_key)
    ref_values = project(ref_rows, w_value)
    piece_keys = lax.all_gather(ref_keys, "frame", axis=0, tiled=True)
    piece_values = lax.all_gather(ref_values, "frame", axis=0, tiled=True)
    count = piece_keys.shape[0]
    heads_k = piece_keys.reshape(count, HEADS, head_dim).transpose(1, 0, 2)
    heads_v = piece_values.reshape(count, HEADS, head_dim).transpose(1, 0, 2)

    def one_head(args):
        qa, peak, total, accum, ka, va = args
        scores = jnp.einsum("fqd,kd->fqk", qa, ka, preferred_element_type=jnp.float32) * scale
        newpeak = jnp.maximum(peak, jnp.max(scores, axis=-1))
        factor = jnp.exp(peak - newpeak)
        expo = jnp.exp(scores - newpeak[..., None])
        total = total * factor + jnp.sum(expo, axis=-1)
        accum = accum * factor[..., None] + jnp.einsum(
            "fqk,kd->fqd", expo.astype(jnp.bfloat16), va, preferred_element_type=jnp.float32
        )
        return (newpeak, total, accum)

    final = lax.map(
        one_head, (query, start_carry[0], start_carry[1], start_carry[2], heads_k, heads_v)
    )
    attended = (
        (final[2] / final[1][..., None])
        .transpose(1, 2, 0, 3)
        .reshape(-1, width)
        .astype(jnp.bfloat16)
    )
    first = (
        frames.astype(jnp.float32)
        + jnp.dot(attended, w_out, preferred_element_type=jnp.float32).reshape(fdev, pixels, width)
    ).astype(jnp.bfloat16)
    padded = padded_2(first, (("frame", 0),), 1)
    conv = jnp.zeros((fdev * pixels, width), jnp.float32)
    for tap in range(3):
        conv = conv + jnp.dot(
            padded[tap : tap + fdev].reshape(-1, width),
            w_conv[tap],
            preferred_element_type=jnp.float32,
        )
    second = (first.astype(jnp.float32) + conv.reshape(fdev, pixels, width)).astype(jnp.bfloat16)
    normed2 = layer_norm(second.astype(jnp.float32)).astype(jnp.bfloat16)
    grouped = normed2.reshape(fdev, ndev, group_px, width)
    features = lax.all_to_all(grouped, "frame", split_axis=1, concat_axis=0, tiled=True)
    nframes, groups, count, channels = features.shape
    flat = features.reshape(-1, channels)
    tquery = project(flat, t_query).reshape(nframes, groups * count, channels)
    tkeys = project(flat, t_key).reshape(nframes, groups * count, channels)
    tvalues = project(flat, t_value).reshape(nframes, groups * count, channels)
    mixed = temporal_attend(tquery, tkeys, tvalues).reshape(nframes, groups, count, channels)
    back = lax.all_to_all(mixed, "frame", split_axis=0, concat_axis=1, tiled=True)
    result = second.astype(jnp.float32) + jnp.dot(
        back.reshape(-1, width), t_out, preferred_element_type=jnp.float32
    ).reshape(fdev, pixels, width)
    return result.astype(jnp.bfloat16)


def solution(mesh):
    return jax.shard_map(
        per_device,
        mesh=mesh,
        in_specs=(
            P(("video", "frame"), None, None),
            P(("video", "frame"), None),
            P(),
            P(),
            P(),
            P(),
            P(),
            P(),
            P(),
            P(),
            P(),
        ),
        out_specs=P(("video", "frame"), None, None),
        check_vma=False,
    )
```

profile of v0, /device:TPU:0, one launch (start us, length us, event | category | flops | bytes accessed | tf_op | source)
XLA Modules:
  0.0 356.0 jit_solution(769306988038147561)
XLA Ops:
  12.7 2.6 convolution_convert_fusion.4
  15.3 2.6 convolution_convert_fusion.3
  20.4 3.5 copy.52
  24.0 3.8 %copy.53 = bf16[1,1024,10,64]{3,1,0,2:T(8,128)(2,1)} copy(bf16[1,1024,10,64]{1,3,2,0:T(8,128)(2,1)} %bitcast.198) | data formatting | bytes 2621440 | tf_op jit(solution)/shard_map/reshape;reshape | solution.py:36
  27.8 3.8 %copy.54 = bf16[1,1024,10,64]{3,1,0,2:T(8,128)(2,1)} copy(bf16[1,1024,10,64]{1,3,2,0:T(8,128)(2,1)} %bitcast.197) | data formatting | bytes 2621440 | tf_op jit(solution)/shard_map/reshape;reshape | solution.py:36
  33.4 49.6 %while.26 = (s32[]{:T(128)}, f32[10,1,1024]{2,1,0:T(1,128)S(1)}, f32[10,1,1024]{2,1,0:T(1,128)S(1)}, f32[10,1,1024,64]{2,3,1,0:T(8,128)}, bf16[10,1,1024,64]{3,2...) while((s32[]{:T(128)}, f32[10,1,1024]{2,1,0:T(1,128)S(1)}, ...), condition=%wide.region_5.6_spmd, body=%wide.region_2.5_spmd.sunk | while | flops 276822016 | bytes 13666393 | solution.py:87
  40.8 2.6 fusion.115
  50.7 2.5 fusion.115
  65.6 2.5 fusion.115
  70.6 2.6 fusion.115
  85.5 11.4 %all-gather.5.cloned.1.call-done = bf16[1024,640]{1,0:T(8,128)(2,1)} async-done(((bf16[128,640]{1,0:T(8,128)(2,1)}), bf16[1024,640]{1,0:T(8,128)(2,1)}) %all-gather.5.cloned.1.call-update) | async-done | bytes 1310736 | tf_op jit(solution)/shard_map/all_gather | solution.py:91
  101.2 51.8 %while.27 = (s32[]{:T(128)}, f32[10,1,1024]{2,0,1:T(8,128)S(1)}, f32[10,1,1024,64]{2,3,1,0:T(8,128)}, f32[10,1,1024]{2,1,0:T(1,128)S(1)}, f32[10,1,1024]{2,1,0:T...) while((s32[]{:T(128)}, f32[10,1,1024]{2,0,1:T(8,128)S(1)}, ...), condition=%wide.region_9.10_spmd, body=%wide.region_6.9_spmd.sunk | while | flops 276959232 | bytes 13707385 | solution.py:108
  102.9 2.6 fusion.119
  108.1 2.6 fusion.119
  113.3 2.6 fusion.119
  118.4 2.6 fusion.119
  123.6 2.6 fusion.119
  128.8 2.6 fusion.119
  134.0 2.6 fusion.119
  139.1 2.6 fusion.119
  144.3 2.6 fusion.119
  149.5 2.6 fusion.119
  162.1 51.6 %collective-permute-done = bf16[1,1024,640]{2,1,0:T(8,128)(2,1)S(1)} collective-permute-done((bf16[1,1024,640]{2,1,0:T(8,128)(2,1)S(1)}, bf16[1,1024,640]{2,1,0:T(8,128)(2,1)S(1)}, u32[]{:S(2)}, u32[]{:S(2)}) %collective-permute-start) | collective-permute-done | bytes 1310752 | tf_op jit(solution)/shard_map/ppermute | solution.py:17
  217.6 36.6 %all_to_all.8 = bf16[1,8,128,640]{3,2,0,1:T(8,128)(2,1)S(1)} all-to-all(bf16[1,8,128,640]{3,2,0,1:T(8,128)(2,1)S(1)} %bitcast.181), channel_id=1, replica_groups=mesh['video'=4,'frame'=8] {'frame'}, dimensions={1} | all-to-all | bytes 2621440 | tf_op jit(solution)/shard_map/all_to_all | solution.py:132
  260.8 7.1 %copy.62 = bf16[8,128,10,64]{3,0,2,1:T(8,128)(2,1)} copy(bf16[8,128,10,64]{1,0,3,2:T(8,128)(2,1)} %bitcast.185) | data formatting | bytes 2621440 | tf_op jit(solution)/shard_map/reshape;reshape | solution.py:42
  273.3 7.1 %copy.63 = bf16[8,128,10,64]{3,0,2,1:T(8,128)(2,1)} copy(bf16[8,128,10,64]{1,0,3,2:T(8,128)(2,1)} %bitcast.186) | data formatting | bytes 2621440 | tf_op jit(solution)/shard_map/reshape;reshape | solution.py:43
  285.8 7.2 %copy.66 = bf16[8,128,10,64]{3,0,2,1:T(8,128)(2,1)} copy(bf16[8,128,10,64]{1,0,3,2:T(8,128)(2,1)} %bitcast.187) | data formatting | bytes 2621440 | tf_op jit(solution)/shard_map/reshape;reshape | solution.py:44
  293.0 4.6 %multiply_reduce_fusion.2 = (f32[128,10,8]{2,1,0:T(8,128)S(1)}, f32[128,10,8,8]{2,3,1,0:T(8,128)S(1)}) fusion(bf16[8,128,10,64]{3,0,2,1:T(8,128)(2,1)} %copy.62, bf16[8,128,10,64]{3,0,2,1:T(8,128)(2,1)} %copy.63), kind=kOutput, calls=%fused_computation.47 | convolution fusion | flops 10639360 | bytes 2990080 | tf_op jit(solution)/shard_map/fnhd,gnhd->nhfg/dot_general | solution.py:45
  299.8 3.9 %fusion.45 = bf16[8,128,10,64]{3,0,2,1:T(8,128)(2,1)} fusion(f32[8,128,10]{0,2,1:T(8,128)S(1)} %bitcast.200, bf16[8,128,10,64]{3,0,2,1:T(8,128)(2,1)S(1)} %copy-done.4, f32[128,10,8,8]{2,3,1,0:T(8,128)S(1)} %get-tuple-element.167, f32[128,10,8]{2,1,0:T(8,128)S(1)} %get-tuple-element.166), kind=kOutput, calls=%fused_computation.45 | convolution fusion | flops 12042240 | bytes 3031040 | tf_op jit(solution)/shard_map/nhfg,gnhd->nhfd/dot_general | solution.py:52
  303.8 5.1 %copy.67 = bf16[8,128,10,64]{1,3,2,0:T(8,128)(2,1)} copy(bf16[8,128,10,64]{3,0,2,1:T(8,128)(2,1)} %fusion.45) | data formatting | bytes 2621440 | tf_op jit(solution)/shard_map/convert_element_type | solution.py:60
  308.9 34.7 %all_to_all.9 = bf16[8,1,128,640]{2,3,1,0:T(8,128)(2,1)S(1)} all-to-all(bf16[8,1,128,640]{2,3,1,0:T(8,128)(2,1)} %bitcast.188), channel_id=1, replica_groups=mesh['video'=4,'frame'=8] {'frame'}, dimensions={0} | all-to-all | bytes 2621440 | tf_op jit(solution)/shard_map/all_to_all | solution.py:139
  345.0 4.0 %fusion.57 = bf16[1,1024,640]{2,1,0:T(8,128)(2,1)} fusion(bf16[1,1024,640]{2,1,0:T(8,128)(2,1)S(1)} %get-tuple-element.165, bf16[1024,640]{1,0:T(8,128)(2,1)} %bitcast.196, bf16[640,640]{1,0:T(8,128)(2,1)} %param.25), kind=kOutput, calls=%fused_computation.65 | convolution fusion | flops 840826880 | bytes 4751360 | tf_op jit(solution)/shard_map/dot_general | solution.py:140
  (168 shorter events, 116.0 us)
Async XLA Ops:
  6.5 1.1 copy-start
  6.5 5.4 %copy-start.2 = (bf16[1,1024,640]{2,1,0:T(8,128)(2,1)S(1)}, bf16[1,1024,640]{2,1,0:T(8,128)(2,1)}, u32[]{:S(2)}) copy-start(bf16[1,1024,640]{2,1,0:T(8,128)(2,1)} %param.15) | copy-start | bytes 3932164
  6.5 76.5 %all-gather.3.cloned.1.call-start = ((), (), s32[]{:S(2)}) async-start(), calls=%async_computation.2 | async-start | bytes 1474560 | tf_op jit(solution)/shard_map/all_gather | solution.py:90
  9.6 87.3 %all-gather.5.cloned.1.call-start = ((), (), s32[]{:S(2)}) async-start(), calls=%async_computation.3 | async-start | bytes 1474560 | tf_op jit(solution)/shard_map/all_gather | solution.py:91
  12.7 2.6 copy-start.8
  15.3 2.6 copy-start.10
  153.0 2.3 copy-start.3
  153.0 2.3 copy-start.11
  155.3 5.5 %copy-start.9 = (bf16[3,640,640]{2,1,0:T(8,128)(2,1)S(1)}, bf16[3,640,640]{2,1,0:T(8,128)(2,1)}, u32[]{:S(2)}) copy-start(bf16[3,640,640]{2,1,0:T(8,128)(2,1)} %param.21) | copy-start | bytes 7372804
  156.8 57.0 %collective-permute-start = (bf16[1,1024,640]{2,1,0:T(8,128)(2,1)S(1)}, bf16[1,1024,640]{2,1,0:T(8,128)(2,1)S(1)}, u32[]{:S(2)}, u32[]{:S(2)}) collective-permute-start(bf16[1,1024,640]{2,1,0:T(8,128)(2,1)S(1)} %fusion.56), channel_id=1, source_target_pairs={{0,1},{1,2},{2,3},{3,4},{4,5},{5,6},{6,7},{8,9},{9,10},{10,11},{11... | collective-permute-start | bytes 3932168 | tf_op jit(solution)/shard_map/ppermute | solution.py:17
  159.3 55.8 %collective-permute-start.1 = (bf16[1,1024,640]{2,1,0:T(8,128)(2,1)S(1)}, bf16[1,1024,640]{2,1,0:T(8,128)(2,1)S(1)}, u32[]{:S(2)}, u32[]{:S(2)}) collective-permute-start(bf16[1,1024,640]{2,1,0:T(8,128)(2,1)S(1)} %fusion.56), channel_id=1, source_target_pairs={{1,0},{2,1},{3,2},{4,3},{5,4},{6,5},{7,6},{9,8},{10,9},{11,10},{12... | collective-permute-start | bytes 3932168 | tf_op jit(solution)/shard_map/ppermute | solution.py:18
  217.2 38.2 %copy-start.12 = (bf16[640,640]{1,0:T(8,128)(2,1)S(1)}, bf16[640,640]{1,0:T(8,128)(2,1)}, u32[]{:S(2)}) copy-start(bf16[640,640]{1,0:T(8,128)(2,1)} %param.22) | copy-start | bytes 2457604
  254.2 1.1 copy-start.5
  260.8 7.1 %copy-start.6 = (bf16[1,8,128,640]{3,2,0,1:T(8,128)(2,1)S(1)}, bf16[1,8,128,640]{3,2,0,1:T(8,128)(2,1)}, u32[]{:S(2)}) copy-start(bf16[1,8,128,640]{3,2,0,1:T(8,128)(2,1)} %copy-done.5) | copy-start | bytes 3932164
  260.8 7.1 %copy-start.13 = (bf16[640,640]{1,0:T(8,128)(2,1)S(1)}, bf16[640,640]{1,0:T(8,128)(2,1)}, u32[]{:S(2)}) copy-start(bf16[640,640]{1,0:T(8,128)(2,1)} %param.23) | copy-start | bytes 2457604
  273.3 7.1 %copy-start.7 = (bf16[1,8,128,640]{3,2,0,1:T(8,128)(2,1)S(1)}, bf16[1,8,128,640]{3,2,0,1:T(8,128)(2,1)}, u32[]{:S(2)}) copy-start(bf16[1,8,128,640]{3,2,0,1:T(8,128)(2,1)} %copy-done.5) | copy-start | bytes 3932164
  273.3 7.1 %copy-start.14 = (bf16[640,640]{1,0:T(8,128)(2,1)S(1)}, bf16[640,640]{1,0:T(8,128)(2,1)}, u32[]{:S(2)}) copy-start(bf16[640,640]{1,0:T(8,128)(2,1)} %param.24) | copy-start | bytes 2457604
  297.6 2.2 copy-start.4
  345.0 4.0 %copy-start.1 = (bf16[640,640]{1,0:T(8,128)(2,1)S(1)}, bf16[640,640]{1,0:T(8,128)(2,1)}, u32[]{:S(2)}) copy-start(bf16[640,640]{1,0:T(8,128)(2,1)} %param.18) | copy-start | bytes 2457604
Sparse Core Ops, SparseCore 0:
  9.7 44.5 all-gather.2
  56.5 40.3 all-gather.4
where the time goes:
time: 362 us; the launch traced here: 356 us
  matrix products  122 us (34%)
  blocking collectives  71.3 us (20%)
  waiting for transfers between devices  63.1 us (17%)
  local copies, waits for them, and re-layouts  60.4 us (17%)
  other arithmetic  21.1 us (6%)
  between operations  13.9 us (4%)
  starting transfers between devices  4.04 us (1%)
    ppermute x1, waiting for transfers between devices, padded_2(): before = lax.ppermute(last, axis, up)  51.6 us
    all_to_all x1, blocking collectives, per_device(): lax.all_to_all(grouped, 'frame', split_axis=1, concat_axis=0, tiled=True)  36.6 us
    all_to_all x1, blocking collectives, per_device(): lax.all_to_all(mixed, 'frame', split_axis=0, concat_axis=1, tiled=True)  34.7 us
    dot_general x10, matrix products, one_head(): jnp.einsum('fqk,kd->fqd', expo.astype(jnp.bfloat16), va, preferred_elemen...  25.7 us
    dot_general x10, matrix products, local_part(): jnp.einsum('fqk,fkd->fqd', expo.astype(jnp.bfloat16), va, preferred_eleme...  25.4 us
    dot_general x8, matrix products, project(): jnp.dot(rows, weight, preferred_element_type=jnp.float32)  18.9 us
    dot_general x10, matrix products, one_head(): jnp.einsum('fqd,kd->fqk', qa, ka, preferred_element_type=jnp.float32)  16.7 us
    dot_general x10, matrix products, local_part(): jnp.einsum('fqd,fkd->fqk', qa, ka, preferred_element_type=jnp.float32)  16.7 us
  transfers between devices with their start and end apart: 4, of which 2 were waited for; matrix products, arithmetic and copies ran while one was open for 22% of the time, Pallas kernels for 0%

commit v1 on v0

--- a/solution.py
+++ b/solution.py
@@ -136,7 +136,10 @@
     tkeys = project(flat, t_key).reshape(nframes, groups * count, channels)
     tvalues = project(flat, t_value).reshape(nframes, groups * count, channels)
     mixed = temporal_attend(tquery, tkeys, tvalues).reshape(nframes, groups, count, channels)
-    back = lax.all_to_all(mixed, "frame", split_axis=0, concat_axis=1, tiled=True)
+    back = jnp.concatenate(
+        lax.all_to_all(jnp.stack(jnp.split(mixed, lax.axis_size("frame"), axis=0)), "frame", 0, 0),
+        axis=1,
+    )
     result = second.astype(jnp.float32) + jnp.dot(
         back.reshape(-1, width), t_out, preferred_element_type=jnp.float32
     ).reshape(fdev, pixels, width)

time: 362 us -> 381 us (1.052)
  local copies, waits for them, and re-layouts: 60.4 us -> 79.8 us
    split x0 -> x9, local copies, waits for them, and re-layouts: none -> 16.3 us  [per_device(): jnp.split(mixed, lax.axis_size('frame'), axis=0)]
    unnamed x33 -> x44, local copies, waits for them, and re-layouts: 6.63 us -> 14.1 us
    convert_element_type x1 -> x0, local copies, waits for them, and re-layouts: 5.1 us -> none  [temporal_attend(): tmixed.transpose(2, 0, 1, 3).reshape(nframes, pixels, width)]
  transfers between devices with their start and end apart: 4 -> 4, of which waited for: 2 -> 2; matrix products, arithmetic and copies ran while one was open for 22% -> 21% of each run, Pallas kernels for 0% -> 0%
where the time goes in v1:
time: 381 us; the launch traced here: 374 us
  matrix products  120 us (31%)
  local copies, waits for them, and re-layouts  79.8 us (21%)
  blocking collectives  71.3 us (19%)
  waiting for transfers between devices  63.3 us (17%)
  other arithmetic  21.1 us (6%)
  between operations  13.9 us (4%)
  starting transfers between devices  4.04 us (1%)
    ppermute x1, waiting for transfers between devices, padded_2(): before = lax.ppermute(last, axis, up)  51.6 us
    all_to_all x1, blocking collectives, per_device(): lax.all_to_all(grouped, 'frame', split_axis=1, concat_axis=0, tiled=True)  36.6 us
    all_to_all x1, blocking collectives, per_device(): lax.all_to_all(jnp.stack(jnp.split(mixed, lax.axis_size('frame'), axis=0)...  34.7 us
    dot_general x10, matrix products, one_head(): jnp.einsum('fqk,kd->fqd', expo.astype(jnp.bfloat16), va, preferred_elemen...  25.7 us
    dot_general x10, matrix products, local_part(): jnp.einsum('fqk,fkd->fqd', expo.astype(jnp.bfloat16), va, preferred_eleme...  25.4 us
    dot_general x8, matrix products, project(): jnp.dot(rows, weight, preferred_element_type=jnp.float32)  18.9 us
    dot_general x10, matrix products, one_head(): jnp.einsum('fqd,kd->fqk', qa, ka, preferred_element_type=jnp.float32)  16.7 us
    dot_general x10, matrix products, local_part(): jnp.einsum('fqd,fkd->fqk', qa, ka, preferred_element_type=jnp.float32)  16.7 us
  transfers between devices with their start and end apart: 4, of which 2 were waited for; matrix products, arithmetic and copies ran while one was open for 21% of the time, Pallas kernels for 0%

profile of v1, /device:TPU:0, one launch (start us, length us, event | category | flops | bytes accessed | tf_op | source)
XLA Modules:
  0.0 374.4 jit_solution(17548948906862651244)
XLA Ops:
  15.3 2.6 convolution_convert_fusion.3
  17.9 2.5 convolution_convert_fusion.5
  20.4 3.5 copy.66
  24.0 3.8 %copy.67 = bf16[1,1024,10,64]{3,1,0,2:T(8,128)(2,1)} copy(bf16[1,1024,10,64]{1,3,2,0:T(8,128)(2,1)} %bitcast.202) | data formatting | bytes 2621440 | tf_op jit(solution)/shard_map/reshape;reshape | solution.py:36
  27.8 3.8 %copy.68 = bf16[1,1024,10,64]{3,1,0,2:T(8,128)(2,1)} copy(bf16[1,1024,10,64]{1,3,2,0:T(8,128)(2,1)} %bitcast.201) | data formatting | bytes 2621440 | tf_op jit(solution)/shard_map/reshape;reshape | solution.py:36
  33.4 49.6 %while.26 = (s32[]{:T(128)}, f32[10,1,1024]{2,1,0:T(1,128)S(1)}, f32[10,1,1024]{2,1,0:T(1,128)S(1)}, f32[10,1,1024,64]{2,3,1,0:T(8,128)}, bf16[10,1,1024,64]{3,2...) while((s32[]{:T(128)}, f32[10,1,1024]{2,1,0:T(1,128)S(1)}, ...), condition=%wide.region_5.6_spmd, body=%wide.region_2.5_spmd.sunk | while | flops 276822016 | bytes 13666393 | solution.py:87
  40.8 2.5 fusion.116
  60.6 2.5 fusion.116
  70.6 2.5 fusion.116
  85.4 11.6 %all-gather.5.cloned.1.call-done = bf16[1024,640]{1,0:T(8,128)(2,1)} async-done(((bf16[128,640]{1,0:T(8,128)(2,1)}), bf16[1024,640]{1,0:T(8,128)(2,1)}) %all-gather.5.cloned.1.call-update) | async-done | bytes 1310736 | tf_op jit(solution)/shard_map/all_gather | solution.py:91
  101.4 51.7 %while.27 = (s32[]{:T(128)}, f32[10,1,1024]{2,0,1:T(8,128)S(1)}, f32[10,1,1024,64]{2,3,1,0:T(8,128)}, f32[10,1,1024]{2,1,0:T(1,128)S(1)}, f32[10,1,1024]{2,1,0:T...) while((s32[]{:T(128)}, f32[10,1,1024]{2,0,1:T(8,128)S(1)}, ...), condition=%wide.region_9.10_spmd, body=%wide.region_6.9_spmd.sunk | while | flops 276959232 | bytes 13707385 | solution.py:108
  103.1 2.6 fusion.120
  108.2 2.6 fusion.120
  113.4 2.6 fusion.120
  118.6 2.6 fusion.120
  123.7 2.6 fusion.120
  128.9 2.6 fusion.120
  134.1 2.6 fusion.120
  139.3 2.6 fusion.120
  144.5 2.6 fusion.120
  149.6 2.6 fusion.120
  156.9 2.5 collective-permute-start
  162.2 51.6 %collective-permute-done = bf16[1,1024,640]{2,1,0:T(8,128)(2,1)S(1)} collective-permute-done((bf16[1,1024,640]{2,1,0:T(8,128)(2,1)S(1)}, bf16[1,1024,640]{2,1,0:T(8,128)(2,1)S(1)}, u32[]{:S(2)}, u32[]{:S(2)}) %collective-permute-start) | collective-permute-done | bytes 1310752 | tf_op jit(solution)/shard_map/ppermute | solution.py:17
  217.7 36.6 %all_to_all.14 = bf16[1,8,128,640]{3,2,0,1:T(8,128)(2,1)S(1)} all-to-all(bf16[1,8,128,640]{3,2,0,1:T(8,128)(2,1)S(1)} %bitcast.186), channel_id=1, replica_groups=mesh['video'=4,'frame'=8] {'frame'}, dimensions={1} | all-to-all | bytes 2621440 | tf_op jit(solution)/shard_map/all_to_all | solution.py:132
  260.9 7.1 %copy.76 = bf16[8,128,10,64]{3,0,2,1:T(8,128)(2,1)} copy(bf16[8,128,10,64]{1,0,3,2:T(8,128)(2,1)} %bitcast.190) | data formatting | bytes 2621440 | tf_op jit(solution)/shard_map/reshape;reshape | solution.py:42
  273.4 7.1 %copy.77 = bf16[8,128,10,64]{3,0,2,1:T(8,128)(2,1)} copy(bf16[8,128,10,64]{1,0,3,2:T(8,128)(2,1)} %bitcast.191) | data formatting | bytes 2621440 | tf_op jit(solution)/shard_map/reshape;reshape | solution.py:43
  285.9 7.1 %copy.80 = bf16[8,128,10,64]{3,0,2,1:T(8,128)(2,1)} copy(bf16[8,128,10,64]{1,0,3,2:T(8,128)(2,1)} %bitcast.192) | data formatting | bytes 2621440 | tf_op jit(solution)/shard_map/reshape;reshape | solution.py:44
  293.1 4.6 %multiply_reduce_fusion.2 = (f32[128,10,8]{2,1,0:T(8,128)S(1)}, f32[128,10,8,8]{2,3,1,0:T(8,128)S(1)}) fusion(bf16[8,128,10,64]{3,0,2,1:T(8,128)(2,1)} %copy.76, bf16[8,128,10,64]{3,0,2,1:T(8,128)(2,1)} %copy.77), kind=kOutput, calls=%fused_computation.47 | convolution fusion | flops 10639360 | bytes 2990080 | tf_op jit(solution)/shard_map/fnhd,gnhd->nhfg/dot_general | solution.py:45
  299.9 2.9 fusion.45
  302.8 5.4 %fusion.84 = (bf16[1,128,10,64]{3,0,2,1:T(2,128)(2,1)S(1)}, bf16[1,128,10,64]{3,0,2,1:T(2,128)(2,1)S(1)}, bf16[1,128,10,64]{3,0,2,1:T(2,128)(2,1)S(1)}, bf16[1,1...) fusion(bf16[8,128,10,64]{3,0,2,1:T(8,128)(2,1)S(1)} %fusion.45), kind=kLoop, calls=%fused_computation.106 | loop fusion | bytes 2621440 | tf_op jit(solution)/shard_map/split | solution.py:140
  327.3 34.7 %all_to_all.15 = bf16[8,1,1,128,640]{3,4,2,1,0:T(8,128)(2,1)S(1)} all-to-all(bf16[8,1,1,128,640]{3,4,2,1,0:T(8,128)(2,1)} %constant_dynamic-update-slice_fusion.2), channel_id=1, replica_groups=mesh['video'=4,'frame'=8] {'frame'}, dimensions={0} | all-to-all | bytes 2621440 | tf_op jit(solution)/shard_map/all_to_all | solution.py:140
  363.4 4.0 %fusion.57 = bf16[1,1024,640]{2,1,0:T(8,128)(2,1)} fusion(bf16[1,1024,640]{2,1,0:T(8,128)(2,1)S(1)} %get-tuple-element.173, bf16[1024,640]{1,0:T(8,128)(2,1)} %bitcast.200, bf16[640,640]{1,0:T(8,128)(2,1)} %param.25), kind=kOutput, calls=%fused_computation.65 | convolution fusion | flops 840826880 | bytes 4751360 | tf_op jit(solution)/shard_map/dot_general | solution.py:143
  (188 shorter events, 134.9 us)
Async XLA Ops:
  6.5 1.1 copy-start
  6.5 5.3 %copy-start.2 = (bf16[1,1024,640]{2,1,0:T(8,128)(2,1)S(1)}, bf16[1,1024,640]{2,1,0:T(8,128)(2,1)}, u32[]{:S(2)}) copy-start(bf16[1,1024,640]{2,1,0:T(8,128)(2,1)} %param.15) | copy-start | bytes 3932164
  6.5 76.5 %all-gather.3.cloned.1.call-start = ((), (), s32[]{:S(2)}) async-start(), calls=%async_computation.2 | async-start | bytes 1474560 | tf_op jit(solution)/shard_map/all_gather | solution.py:90
  9.6 87.5 %all-gather.5.cloned.1.call-start = ((), (), s32[]{:S(2)}) async-start(), calls=%async_computation.3 | async-start | bytes 1474560 | tf_op jit(solution)/shard_map/all_gather | solution.py:91
  12.7 2.5 copy-start.8
  15.3 2.6 copy-start.12
  153.1 2.3 copy-start.3
  153.1 2.3 copy-start.13
  155.4 5.5 %copy-start.11 = (bf16[3,640,640]{2,1,0:T(8,128)(2,1)S(1)}, bf16[3,640,640]{2,1,0:T(8,128)(2,1)}, u32[]{:S(2)}) copy-start(bf16[3,640,640]{2,1,0:T(8,128)(2,1)} %param.21) | copy-start | bytes 7372804
  156.9 57.0 %collective-permute-start = (bf16[1,1024,640]{2,1,0:T(8,128)(2,1)S(1)}, bf16[1,1024,640]{2,1,0:T(8,128)(2,1)S(1)}, u32[]{:S(2)}, u32[]{:S(2)}) collective-permute-start(bf16[1,1024,640]{2,1,0:T(8,128)(2,1)S(1)} %fusion.56), channel_id=1, source_target_pairs={{0,1},{1,2},{2,3},{3,4},{4,5},{5,6},{6,7},{8,9},{9,10},{10,11},{11... | collective-permute-start | bytes 3932168 | tf_op jit(solution)/shard_map/ppermute | solution.py:17
  159.4 55.8 %collective-permute-start.1 = (bf16[1,1024,640]{2,1,0:T(8,128)(2,1)S(1)}, bf16[1,1024,640]{2,1,0:T(8,128)(2,1)S(1)}, u32[]{:S(2)}, u32[]{:S(2)}) collective-permute-start(bf16[1,1024,640]{2,1,0:T(8,128)(2,1)S(1)} %fusion.56), channel_id=1, source_target_pairs={{1,0},{2,1},{3,2},{4,3},{5,4},{6,5},{7,6},{9,8},{10,9},{11,10},{12... | collective-permute-start | bytes 3932168 | tf_op jit(solution)/shard_map/ppermute | solution.py:18
  217.3 38.2 %copy-start.14 = (bf16[640,640]{1,0:T(8,128)(2,1)S(1)}, bf16[640,640]{1,0:T(8,128)(2,1)}, u32[]{:S(2)}) copy-start(bf16[640,640]{1,0:T(8,128)(2,1)} %param.22) | copy-start | bytes 2457604
  254.3 1.1 copy-start.5
  260.9 7.1 %copy-start.6 = (bf16[1,8,128,640]{3,2,0,1:T(8,128)(2,1)S(1)}, bf16[1,8,128,640]{3,2,0,1:T(8,128)(2,1)}, u32[]{:S(2)}) copy-start(bf16[1,8,128,640]{3,2,0,1:T(8,128)(2,1)} %copy-done.5) | copy-start | bytes 3932164
  260.9 7.1 %copy-start.15 = (bf16[640,640]{1,0:T(8,128)(2,1)S(1)}, bf16[640,640]{1,0:T(8,128)(2,1)}, u32[]{:S(2)}) copy-start(bf16[640,640]{1,0:T(8,128)(2,1)} %param.23) | copy-start | bytes 2457604
  273.4 7.1 %copy-start.7 = (bf16[1,8,128,640]{3,2,0,1:T(8,128)(2,1)S(1)}, bf16[1,8,128,640]{3,2,0,1:T(8,128)(2,1)}, u32[]{:S(2)}) copy-start(bf16[1,8,128,640]{3,2,0,1:T(8,128)(2,1)} %copy-done.5) | copy-start | bytes 3932164
  273.4 7.1 %copy-start.16 = (bf16[640,640]{1,0:T(8,128)(2,1)S(1)}, bf16[640,640]{1,0:T(8,128)(2,1)}, u32[]{:S(2)}) copy-start(bf16[640,640]{1,0:T(8,128)(2,1)} %param.24) | copy-start | bytes 2457604
  297.7 2.2 copy-start.4
  318.8 5.7 %copy-start.10 = (bf16[1,128,10,64]{1,3,2,0:T(8,128)(2,1)S(1)}, bf16[1,128,10,64]{1,3,2,0:T(8,128)(2,1)}, u32[]{:S(2)}) copy-start(bf16[1,128,10,64]{1,3,2,0:T(8,128)(2,1)} %copy.85) | copy-start | bytes 491524
  318.8 6.4 %copy-start.9 = (bf16[1,128,10,64]{1,3,2,0:T(8,128)(2,1)S(1)}, bf16[1,128,10,64]{1,3,2,0:T(8,128)(2,1)}, u32[]{:S(2)}) copy-start(bf16[1,128,10,64]{1,3,2,0:T(8,128)(2,1)} %copy.86) | copy-start | bytes 491524
  363.4 4.0 %copy-start.1 = (bf16[640,640]{1,0:T(8,128)(2,1)S(1)}, bf16[640,640]{1,0:T(8,128)(2,1)}, u32[]{:S(2)}) copy-start(bf16[640,640]{1,0:T(8,128)(2,1)} %param.18) | copy-start | bytes 2457604
Sparse Core Ops, SparseCore 0:
  9.7 44.5 all-gather.2
  56.5 40.5 all-gather.4
